TPU v7x, 32 devices: a whole 2x2x4 slice. The times are simulated.
32 devices in a mesh: seq: 8 (over y, x, core), dp: 4 (over z).
Axes of the slice: x: 2, y: 2, z: 4, core: 2. Of those that a mesh axis runs over, the one named last changes fastest.
Arguments:
- layer_input: bfloat16 [4, 1024, 5120], P('dp', 'seq'), may hold values from -64 to 64, as said below
- out_grad: bfloat16 [4, 1024, 5120], P('dp', 'seq'), may hold values from -0.059814453 to 0.059814453
- w_query: bfloat16 [5120, 640], replicated, may hold values from -0.078125 to 0.078125
- w_key: bfloat16 [5120, 128], replicated, may hold values from -0.078125 to 0.078125
- w_value: bfloat16 [5120, 128], replicated, may hold values from -0.078125 to 0.078125
- w_output: bfloat16 [640, 5120], replicated, may hold values from -0.25 to 0.25
- block_mask: int32 [4, 8, 8], P('dp'), may hold values from 0 to 1, as said below
Outputs:
- grad_qkv: float32 [5120, 896], P(('seq', 'dp'))
- grad_output: float32 [640, 5120], P(('seq', 'dp'))
Inputs may be any that keep to these rules, and one draw needn't show every extreme that they name: `layer_input`: each position's entries are a bell-shaped or uniform body times a scale of that position; they may share a common direction, and some positions may repeat one strong vector. block_mask[r] has ones on its diagonal and zeros above it. The 8 blocks of sequence r form a shared prefix of at least half of them followed by a chosen branch and then a rejected branch, each of one block or more; a block attends every earlier or equal block of the prefix and of its own branch, and nothing else.
All inputs are finite; a program needn't handle non-finite values.
Results may differ from a plain program's by a relative error of at most 0.025.
The roundings to bfloat16 on the way count: a program that leaves them out, or rounds other values in their place, can miss the bound.
Values may be sent and summed in bfloat16 or wider, within the bound.
A program may use at most 128 MiB of HBM per device.

v0:
```python
import math
import jax
import jax.numpy as jnp
from jax import lax
from jax.sharding import PartitionSpec as P

BLOCK = 128


def allowed_block(mask_table, first_row, row_count, length):
    query_pos = first_row + jnp.arange(row_count, dtype=jnp.int32)
    key_pos = jnp.arange(length, dtype=jnp.int32)
    mask_rows = lax.dynamic_slice_in_dim(mask_table, first_row // BLOCK, row_count // BLOCK, 0)
    token_mask = jnp.repeat(jnp.repeat(mask_rows, BLOCK, axis=0), BLOCK, axis=1)
    same_block = query_pos[:, None] // BLOCK == key_pos[None, :] // BLOCK
    return (token_mask == 1) & (
        jnp.logical_not(same_block) | (key_pos[None, :] <= query_pos[:, None])
    )


def shards(layer_input, out_grad, w_query, w_key, w_value, w_output, block_mask):
    inputs_row = layer_input[0]
    grad_row = out_grad[0]
    mask_table = block_mask[0]
    tokens = inputs_row.shape[0]
    head_size = w_key.shape[1]
    group_heads = w_query.shape[1] // head_size
    scale = 1.0 / math.sqrt(head_size)
    queries = (
        jnp.dot(inputs_row, w_query, preferred_element_type=jnp.float32)
        .astype(jnp.bfloat16)
        .reshape(tokens, group_heads, head_size)
    )
    w_pair = jnp.concatenate([w_key, w_value], axis=1)
    kv_local = jnp.dot(inputs_row, w_pair, preferred_element_type=jnp.float32).astype(jnp.bfloat16)
    kv_all = lax.all_gather(kv_local, "seq", axis=0, tiled=True)
    length = kv_all.shape[0]
    key_rows = kv_all[:, :head_size]
    value_rows = kv_all[:, head_size:]
    first_row = lax.axis_index("seq") * tokens
    allowed = allowed_block(mask_table, first_row, tokens, length)
    attn_grad = (
        lax.dot_general(
            grad_row, w_output, (((1,), (1,)), ((), ())), preferred_element_type=jnp.float32
        )
        .astype(jnp.bfloat16)
        .reshape(tokens, group_heads, head_size)
    )
    scores = (
        jnp.einsum("tgh,sh->gts", queries, key_rows, preferred_element_type=jnp.float32) * scale
    )
    masked = jnp.where(allowed[None], scores, -jnp.inf)
    row_max = jnp.max(masked, axis=-1, keepdims=True)
    log_total = row_max + jnp.log(jnp.sum(jnp.exp(masked - row_max), axis=-1, keepdims=True))
    softmax_w = jnp.exp(masked - log_total)
    weights_b = softmax_w.astype(jnp.bfloat16)
    attn_out = jnp.einsum(
        "gts,sh->tgh", weights_b, value_rows, preferred_element_type=jnp.float32
    ).astype(jnp.bfloat16)
    row_delta = jnp.einsum(
        "tgh,tgh->gt", attn_grad.astype(jnp.float32), attn_out.astype(jnp.float32)
    )
    prob_grad = jnp.einsum("tgh,sh->gts", attn_grad, value_rows, preferred_element_type=jnp.float32)
    score_grad = (softmax_w * (prob_grad - row_delta[..., None])).astype(jnp.bfloat16)
    query_grad = (
        jnp.einsum("gts,sh->tgh", score_grad, key_rows, preferred_element_type=jnp.float32) * scale
    ).astype(jnp.bfloat16)
    query_grad = query_grad.reshape(tokens, group_heads * head_size)
    key_term = (
        jnp.einsum("gts,tgh->sh", score_grad, queries, preferred_element_type=jnp.float32) * scale
    )
    value_term = jnp.einsum("gts,tgh->sh", weights_b, attn_grad, preferred_element_type=jnp.float32)
    kv_grads = lax.psum_scatter(
        jnp.concatenate([key_term, value_term], axis=1), "seq", scatter_dimension=0, tiled=True
    )
    grads_all = jnp.concatenate([query_grad, kv_grads.astype(jnp.bfloat16)], axis=1)
    attn_flat = attn_out.reshape(tokens, group_heads * head_size)
    contract_rows = (((0,), (0,)), ((), ()))
    inputs_cols, grad_cols = (
        lax.all_to_all(inputs_row, "seq", split_axis=1, concat_axis=0, tiled=True),
        lax.all_to_all(grad_row, "seq", split_axis=1, concat_axis=0, tiled=True),
    )
    grads_seq, attn_seq = (
        lax.all_gather(grads_all, "seq", axis=0, tiled=True),
        lax.all_gather(attn_flat, "seq", axis=0, tiled=True),
    )
    qkv_cols = lax.dot_general(
        inputs_cols, grads_seq, contract_rows, preferred_element_type=jnp.float32
    )
    out_cols = lax.dot_general(
        attn_seq, grad_cols, contract_rows, preferred_element_type=jnp.float32
    )
    out_heads = lax.all_to_all(out_cols, "seq", split_axis=0, concat_axis=1, tiled=True)
    qkv_grad, output_grad = (
        lax.psum_scatter(qkv_cols, "dp", scatter_dimension=0, tiled=True),
        lax.psum_scatter(out_heads, "dp", scatter_dimension=0, tiled=True),
    )
    return (qkv_grad, output_grad)


def solution(mesh):
    placed = (P("dp", "seq", None), P("dp", "seq", None), P(), P(), P(), P(), P("dp", None, None))
    return jax.shard_map(
        shards,
        mesh=mesh,
        in_specs=placed,
        out_specs=(P(("seq", "dp"), None), P(("seq", "dp"), None)),
        check_vma=False,
    )
```

profile of v0, /device:TPU:0, one launch (start us, length us, event | category | flops | bytes accessed | tf_op | source)
XLA Modules:
  0.0 234.5 jit_solution(2066719553764132672)
XLA Ops:
  7.2 0.0 reduce-scatter.7.cloned.1.call-start
  7.3 5.5 %fusion.18 = bf16[128,640]{1,0:T(8,128)(2,1)S(1)} fusion(bf16[640,5120]{1,0:T(8,128)(2,1)} %param.12, bf16[1,128,5120]{2,1,0:T(8,128)(2,1)} %param.8), kind=kOutput, calls=%fused_computation.23 | convolution fusion | flops 838942720 | bytes 8028160 | tf_op jit(solution)/shard_map/dot_general | solution.py:43
  12.8 0.2 copy.46
  12.9 4.2 %fusion.15 = bf16[128,640]{1,0:T(8,128)(2,1)S(1)} fusion(bf16[5120,640]{1,0:T(8,128)(2,1)} %param.9, bf16[1,128,5120]{2,1,0:T(8,128)(2,1)S(1)} %copy-done), kind=kOutput, calls=%fused_computation.22 | convolution fusion | flops 838942720 | bytes 8028160 | tf_op jit(solution)/shard_map/dot_general | solution.py:30
  17.1 0.2 copy.43
  17.3 2.2 fusion.26
  19.5 11.4 %all_gather.9 = bf16[1024,256]{0,1:T(8,128)(2,1)S(1)} all-gather(bf16[128,256]{0,1:T(8,128)(2,1)S(1)} %fusion.26), channel_id=1, replica_groups=mesh['seq'=8,'dp'=4] {'seq'}, dimensions={0}, use_global_device_ids=true | all-gather | bytes 589824 | tf_op jit(solution)/shard_map/all_gather | solution.py:36
  31.0 0.7 compare_bitcast_fusion
  31.6 0.1 broadcast_bitcast_fusion
  31.7 0.3 fusion.32
  32.1 0.6 fusion.40
  32.6 0.4 exponential_reduce_fusion
  33.0 0.6 convolution_bitcast_fusion.1
  33.6 1.3 fusion.35
  34.9 0.7 fusion.6
  35.6 0.5 fusion.13
  36.1 1.1 pad_maximum_fusion
  37.2 0.0 reduce-scatter.7.cloned.1.call-update
  37.2 0.0 all-gather.3.cloned.1.call-start
  37.3 0.4 fusion.14
  37.6 36.1 %reduce-scatter.7.cloned.1.call-done = f32[128,256]{0,1:T(8,128)} async-done(((f32[1024,256]{0,1:T(8,128)}), f32[128,256]{0,1:T(8,128)}) %reduce-scatter.7.cloned.1.call-update) | async-done | bytes 131088 | tf_op jit(solution)/shard_map/reduce_scatter | solution.py:73
  73.7 0.9 convert_element_type.45
  74.6 0.7 pad_maximum_fusion.1
  75.4 0.0 all-gather.5.cloned.1.call-start
  75.4 0.7 all-gather.5.cloned.1.call-update
  76.1 1.4 copy.53
  77.6 3.7 %all-to-all-start = ((bf16[128,8,640]{0,2,1:T(8,128)(2,1)}), bf16[128,8,640]{0,2,1:T(8,128)(2,1)S(1)}, u32[]{:S(2)}, u32[]{:S(2)}) async-start(bf16[128,8,640]{0,2,1:T(8,128)(2,1)} %bitcast.23), calls=%async_computation.1 | async-start | bytes 2621440 | tf_op jit(solution)/shard_map/all_to_all | solution.py:80
  81.3 0.2 copy.80
  81.5 1.2 copy.55
  82.7 19.2 %all-to-all-done = bf16[128,8,640]{0,2,1:T(8,128)(2,1)S(1)} async-done(((bf16[128,8,640]{0,2,1:T(8,128)(2,1)}), bf16[128,8,640]{0,2,1:T(8,128)(2,1)S(1)}, u32[]{:S(2)}, u32[]{:S(2)}) %all-to-all-start) | async-done | bytes 1310752 | tf_op jit(solution)/shard_map/all_to_all | solution.py:80
  101.9 4.3 %all-to-all-start.1 = ((bf16[128,8,640]{2,0,1:T(8,128)(2,1)}), bf16[128,8,640]{2,0,1:T(8,128)(2,1)}, u32[]{:S(2)}, u32[]{:S(2)}) async-start(bf16[128,8,640]{2,0,1:T(8,128)(2,1)} %copy.55), calls=%async_computation.2 | async-start | bytes 2621440 | tf_op jit(solution)/shard_map/all_to_all | solution.py:81
  106.2 0.0 reduce-scatter.9.cloned.1.call-start
  106.2 1.4 copy.54
  107.6 1.0 all-gather.3.cloned.1.call-done
  108.7 3.5 %convolution_bitcast_fusion = f32[640,896]{0,1:T(8,128)S(1)} fusion(bf16[1024,896]{0,1:T(8,128)(2,1)} %all-gather.3.cloned.1.call-done, bf16[1024,640]{1,0:T(8,128)(2,1)} %bitcast.108), kind=kOutput, calls=%fused_computation.11 | convolution fusion | flops 1174405120 | bytes 5439488 | tf_op jit(solution)/shard_map/dot_general | solution.py:87
  112.1 2.1 copy.76
  114.2 0.0 reduce-scatter.9.cloned.1.call-update
  114.2 11.9 %all-to-all-done.1 = bf16[128,8,640]{2,0,1:T(8,128)(2,1)} async-done(((bf16[128,8,640]{2,0,1:T(8,128)(2,1)}), bf16[128,8,640]{2,0,1:T(8,128)(2,1)}, u32[]{:S(2)}, u32[]{:S(2)}) %all-to-all-start.1) | async-done | bytes 1310752 | tf_op jit(solution)/shard_map/all_to_all | solution.py:81
  126.2 10.7 %all-gather.5.cloned.1.call-done = bf16[1024,640]{0,1:T(8,128)(2,1)} async-done(((bf16[128,640]{0,1:T(8,128)(2,1)}), bf16[1024,640]{0,1:T(8,128)(2,1)}) %all-gather.5.cloned.1.call-update) | async-done | bytes 1310736 | tf_op jit(solution)/shard_map/all_gather | solution.py:85
  136.8 2.9 %fusion.41 = f32[8,80,640]{2,1,0:T(8,128)S(1)} fusion(bf16[8,80,1024]{2,1,0:T(8,128)(2,1)} %bitcast.113, bf16[1024,640,1]{1,0,2:T(8,128)(2,1)} %bitcast.32), kind=kOutput, calls=%fused_computation.54 | convolution fusion | flops 838860800 | bytes 4259840 | tf_op jit(solution)/shard_map/dot_general | solution.py:90
  139.7 24.2 %all_to_all.54 = f32[8,80,640]{2,1,0:T(8,128)S(1)} all-to-all(f32[8,80,640]{2,1,0:T(8,128)S(1)} %fusion.41), channel_id=1, replica_groups=mesh['seq'=8,'dp'=4] {'seq'}, dimensions={0} | all-to-all | bytes 3276800 | tf_op jit(solution)/shard_map/all_to_all | solution.py:93
  164.0 0.1 copy.79
  164.1 54.3 %fusion = f32[24,5120]{1,0:T(8,128)S(1)} fusion(f32[80,5120]{1,0:T(8,128)S(1)} %bitcast.101), kind=kCustom, calls=%all-reduce-scatter | all-reduce-scatter fusion | flops 491521 | bytes 2130432
  218.4 1.3 collective-permute-start
  219.8 0.6 dynamic-slice.5
  221.0 5.6 %collective-permute-done = f32[12,5120]{1,0:T(8,128)S(1)} collective-permute-done((f32[12,5120]{1,0:T(8,128)S(1)}, f32[12,5120]{1,0:T(8,128)S(1)}, u32[]{:S(2)}, u32[]{:S(2)}) %collective-permute-start) | collective-permute-done | bytes 245792
  226.7 0.5 concatenate.12
  227.2 0.8 constant_dynamic-slice_fusion
  (14 shorter events, 0.1 us)
Async XLA Ops:
  7.2 66.6 %reduce-scatter.7.cloned.1.call-start = ((), (), s32[]{:S(2)}) async-start(), calls=%async_computation.5 | async-start | bytes 1179648 | tf_op jit(solution)/shard_map/reduce_scatter | solution.py:73
  7.2 5.7 %copy-start = (bf16[1,128,5120]{2,1,0:T(8,128)(2,1)S(1)}, bf16[1,128,5120]{2,1,0:T(8,128)(2,1)}, u32[]{:S(2)}) copy-start(bf16[1,128,5120]{2,1,0:T(8,128)(2,1)} %param.7) | copy-start | bytes 3932164
  12.9 4.3 %copy-start.3 = (bf16[5120,128]{1,0:T(8,128)(2,1)S(1)}, bf16[5120,128]{1,0:T(8,128)(2,1)}, u32[]{:S(2)}) copy-start(bf16[5120,128]{1,0:T(8,128)(2,1)} %param.11) | copy-start | bytes 3932164
  37.2 71.4 %all-gather.3.cloned.1.call-start = ((), (), s32[]{:S(2)}) async-start(), calls=%async_computation.6 | async-start | bytes 2064384 | tf_op jit(solution)/shard_map/all_gather | solution.py:84
  75.4 61.5 %all-gather.5.cloned.1.call-start = ((), (), s32[]{:S(2)}) async-start(), calls=%async_computation.7 | async-start | bytes 1474560 | tf_op jit(solution)/shard_map/all_gather | solution.py:85
  77.6 3.7 %copy-start.1 = (bf16[1,128,5120]{2,1,0:T(8,128)(2,1)S(1)}, bf16[1,128,5120]{2,1,0:T(8,128)(2,1)}, u32[]{:S(2)}) copy-start(bf16[1,128,5120]{2,1,0:T(8,128)(2,1)} %param.8) | copy-start | bytes 3932164
  77.6 24.3 %all-to-all-start = ((bf16[128,8,640]{0,2,1:T(8,128)(2,1)}), bf16[128,8,640]{0,2,1:T(8,128)(2,1)S(1)}, u32[]{:S(2)}, u32[]{:S(2)}) async-start(bf16[128,8,640]{0,2,1:T(8,128)(2,1)} %bitcast.23), calls=%async_computation.1 | async-start | bytes 2621440 | tf_op jit(solution)/shard_map/all_to_all | solution.py:80
  101.9 24.3 %all-to-all-start.1 = ((bf16[128,8,640]{2,0,1:T(8,128)(2,1)}), bf16[128,8,640]{2,0,1:T(8,128)(2,1)}, u32[]{:S(2)}, u32[]{:S(2)}) async-start(bf16[128,8,640]{2,0,1:T(8,128)(2,1)} %copy.55), calls=%async_computation.2 | async-start | bytes 2621440 | tf_op jit(solution)/shard_map/all_to_all | solution.py:81
  106.2 121.8 %reduce-scatter.9.cloned.1.call-start = ((), (), s32[]{:S(2)}) async-start(), calls=%async_computation.8 | async-start | bytes 2867200
  164.1 55.7 %copy-start.2 = (u32[32]{0:T(128)S(1)}, u32[32]{0:T(128)}, u32[]{:S(2)}) copy-start(u32[32]{0:T(128)} %constant.62) | copy-start | bytes 388
  218.4 8.2 %collective-permute-start = (f32[12,5120]{1,0:T(8,128)S(1)}, f32[12,5120]{1,0:T(8,128)S(1)}, u32[]{:S(2)}, u32[]{:S(2)}) collective-permute-start(f32[12,5120]{1,0:T(8,128)S(1)} %slice.10), channel_id=1, source_target_pairs={{0,1},{1,2},{2,3},{4,5},{5,6},{6,7},{8,9},{9,10},{10,11},{12,13},{... | collective-permute-start | bytes 737288
Sparse Core Ops, SparseCore 0:
  37.3 36.3 reduce-scatter.6
  76.2 32.4 all-gather.2
  110.5 26.2 all-gather.4
  139.6 58.8 reduce-scatter.8
where the time goes:
time: 235 us
  blocking collectives  90 us (38%)
  waiting for transfers between devices  85.2 us (36%)
  matrix products  22.2 us (9%)
  between operations  14.6 us (6%)
  starting transfers between devices  9.44 us (4%)
  local copies, waits for them, and re-layouts  8.93 us (4%)
  other arithmetic  4.09 us (2%)
    unnamed x1, blocking collectives  54.3 us
    reduce_scatter x1, waiting for transfers between devices, shards(): lax.psum_scatter(jnp.concatenate([key_term, value_term], axis=1), 'seq',...  36.1 us
    all_to_all x1, blocking collectives, shards(): lax.all_to_all(out_cols, 'seq', split_axis=0, concat_axis=1, tiled=True)  24.2 us
    all_to_all x1, waiting for transfers between devices, shards(): lax.all_to_all(inputs_row, 'seq', split_axis=1, concat_axis=0, tiled=True)  19.2 us
    all_to_all x1, waiting for transfers between devices, shards(): lax.all_to_all(grad_row, 'seq', split_axis=1, concat_axis=0, tiled=True)  11.9 us
    all_gather x1, blocking collectives, shards(): kv_all = lax.all_gather(kv_local, 'seq', axis=0, tiled=True)  11.4 us
    all_gather x1, waiting for transfers between devices, shards(): lax.all_gather(attn_flat, 'seq', axis=0, tiled=True)  10.7 us
    unnamed x6, waiting for transfers between devices  6.38 us
  transfers between devices with their start and end apart: 7, of which 6 were waited for; matrix products, arithmetic and copies ran while one was open for 30% of the time, Pallas kernels for 0%

commit v1 on v0

--- a/solution.py
+++ b/solution.py
@@ -5,6 +5,16 @@
 from jax.sharding import PartitionSpec as P
 
 BLOCK = 128
+
+
+def gather_by_hops(x, name, dim):
+    peers = lax.axis_size(name)
+    block, tiles = (x, [x])
+    for _ in range(peers - 1):
+        block = lax.ppermute(block, name, [(i, (i + 1) % peers) for i in range(peers)])
+        tiles.insert(0, block)
+    line = jnp.concatenate(tiles, axis=dim)
+    return jnp.roll(line, (lax.axis_index(name) + 1) * x.shape[dim], axis=dim)
 
 
 def allowed_block(mask_table, first_row, row_count, length):
@@ -33,7 +43,7 @@
     )
     w_pair = jnp.concatenate([w_key, w_value], axis=1)
     kv_local = jnp.dot(inputs_row, w_pair, preferred_element_type=jnp.float32).astype(jnp.bfloat16)
-    kv_all = lax.all_gather(kv_local, "seq", axis=0, tiled=True)
+    kv_all = gather_by_hops(kv_local, "seq", 0)
     length = kv_all.shape[0]
     key_rows = kv_all[:, :head_size]
     value_rows = kv_all[:, head_size:]

time: 235 us -> 247 us (1.051)
  waiting for transfers between devices: 85.2 us -> 106 us
  blocking collectives: 90 us -> 78.9 us
    ppermute x0 -> x7, waiting for transfers between devices: none -> 22.5 us  [gather_by_hops(): lax.ppermute(block, name, [(i, (i + 1) % peers) for i in range(peers)])]
    all_gather x1 -> x0, blocking collectives: 11.4 us -> none  [shards(): kv_all = lax.all_gather(kv_local, 'seq', axis=0, tiled=True)]
    dot_general x1, matrix products: 5.48 us -> 2.14 us  [shards(): lax.dot_general(grad_row, w_output, (((1,), (1,)), ((), ())), preferred_e...]
    all_to_all x1, waiting for transfers between devices: 11.9 us -> 8.65 us  [shards(): lax.all_to_all(grad_row, 'seq', split_axis=1, concat_axis=0, tiled=True)]
    unnamed x15 -> x36, local copies, waits for them, and re-layouts: 5.74 us -> 6.93 us
  transfers between devices with their start and end apart: 7 -> 14, of which waited for: 6 -> 13; matrix products, arithmetic and copies ran while one was open for 30% -> 33% of each run, Pallas kernels for 0% -> 0%
where the time goes in v1:
time: 247 us; the launch traced here: 246 us
  waiting for transfers between devices  106 us (43%)
  blocking collectives  78.9 us (32%)
  matrix products  21.5 us (9%)
  between operations  14.8 us (6%)
  starting transfers between devices  11.1 us (4%)
  local copies, waits for them, and re-layouts  10.2 us (4%)
  other arithmetic  4.12 us (2%)
    unnamed x1, blocking collectives  54.7 us
    reduce_scatter x1, waiting for transfers between devices, shards(): lax.psum_scatter(jnp.concatenate([key_term, value_term], axis=1), 'seq',...  35.8 us
    all_to_all x1, blocking collectives, shards(): lax.all_to_all(out_cols, 'seq', split_axis=0, concat_axis=1, tiled=True)  24.2 us
    ppermute x7, waiting for transfers between devices, gather_by_hops(): lax.ppermute(block, name, [(i, (i + 1) % peers) for i in range(peers)])  22.5 us
    all_to_all x1, waiting for transfers between devices, shards(): lax.all_to_all(inputs_row, 'seq', split_axis=1, concat_axis=0, tiled=True)  19.2 us
    all_gather x1, waiting for transfers between devices, shards(): lax.all_gather(attn_flat, 'seq', axis=0, tiled=True)  11.4 us
    all_to_all x1, waiting for transfers between devices, shards(): lax.all_to_all(grad_row, 'seq', split_axis=1, concat_axis=0, tiled=True)  8.65 us
    unnamed x36, local copies, waits for them, and re-layouts  6.93 us
  transfers between devices with their start and end apart: 14, of which 13 were waited for; matrix products, arithmetic and copies ran while one was open for 33% of the time, Pallas kernels for 0%

profile of v1, /device:TPU:0, one launch (start us, length us, event | category | flops | bytes accessed | tf_op | source)
XLA Modules:
  0.0 246.2 jit_solution(14328379050083052800)
XLA Ops:
  7.2 2.8 %fusion.26 = bf16[128,256]{1,0:T(8,128)(2,1)S(1)} fusion(bf16[5120,128]{1,0:T(8,128)(2,1)} %param.11, bf16[5120,128]{1,0:T(8,128)(2,1)} %param.10, bf16[1,128,5120]{2,1,0:T(8,128)(2,1)} %param.7), kind=kOutput, calls=%fused_computation.26 | convolution fusion | flops 340819968 | bytes 3997696 | tf_op jit(solution)/shard_map/dot_general | solution.py:45
  10.0 0.5 collective-permute-start
  10.5 4.3 %fusion.15 = bf16[128,640]{1,0:T(8,128)(2,1)S(1)} fusion(bf16[5120,640]{1,0:T(8,128)(2,1)} %param.9, bf16[1,128,5120]{2,1,0:T(8,128)(2,1)S(1)} %copy-done), kind=kOutput, calls=%fused_computation.22 | convolution fusion | flops 838942720 | bytes 8028160 | tf_op jit(solution)/shard_map/dot_general | solution.py:40
  14.8 0.6 collective-permute-done
  15.4 1.9 collective-permute-start.1
  17.3 2.1 fusion.18
  19.4 0.5 collective-permute-done.1
  20.0 0.7 compare_bitcast_fusion
  20.7 3.9 %collective-permute-done.2 = bf16[128,256]{1,0:T(8,128)(2,1)S(1)} collective-permute-done((bf16[128,256]{1,0:T(8,128)(2,1)S(1)}, bf16[128,256]{1,0:T(8,128)(2,1)S(1)}, u32[]{:S(2)}, u32[]{:S(2)}) %collective-permute-start.2) | collective-permute-done | bytes 65568 | tf_op jit(solution)/shard_map/ppermute | solution.py:14
  24.6 4.5 %collective-permute-done.3 = bf16[128,256]{1,0:T(8,128)(2,1)S(1)} collective-permute-done((bf16[128,256]{1,0:T(8,128)(2,1)S(1)}, bf16[128,256]{1,0:T(8,128)(2,1)S(1)}, u32[]{:S(2)}, u32[]{:S(2)}) %collective-permute-start.3) | collective-permute-done | bytes 65568 | tf_op jit(solution)/shard_map/ppermute | solution.py:14
  29.1 4.6 %collective-permute-done.4 = bf16[128,256]{1,0:T(8,128)(2,1)S(1)} collective-permute-done((bf16[128,256]{1,0:T(8,128)(2,1)S(1)}, bf16[128,256]{1,0:T(8,128)(2,1)S(1)}, u32[]{:S(2)}, u32[]{:S(2)}) %collective-permute-start.4) | collective-permute-done | bytes 65568 | tf_op jit(solution)/shard_map/ppermute | solution.py:14
  33.7 4.6 %collective-permute-done.5 = bf16[128,256]{1,0:T(8,128)(2,1)S(1)} collective-permute-done((bf16[128,256]{1,0:T(8,128)(2,1)S(1)}, bf16[128,256]{1,0:T(8,128)(2,1)S(1)}, u32[]{:S(2)}, u32[]{:S(2)}) %collective-permute-start.5) | collective-permute-done | bytes 65568 | tf_op jit(solution)/shard_map/ppermute | solution.py:14
  38.3 0.3 fusion.32
  38.7 0.2 copy.45
  38.8 0.2 copy.43
  39.0 3.9 %collective-permute-done.6 = bf16[128,256]{1,0:T(8,128)(2,1)S(1)} collective-permute-done((bf16[128,256]{1,0:T(8,128)(2,1)S(1)}, bf16[128,256]{1,0:T(8,128)(2,1)S(1)}, u32[]{:S(2)}, u32[]{:S(2)}) %collective-permute-start.6) | collective-permute-done | bytes 65568 | tf_op jit(solution)/shard_map/ppermute | solution.py:14
  43.1 0.5 fusion.42
  43.7 0.4 exponential_reduce_fusion
  44.0 0.6 convolution_bitcast_fusion.1
  44.6 1.3 fusion.35
  45.9 0.7 fusion.6
  46.6 0.6 fusion.13
  47.1 1.1 pad_maximum_fusion
  48.3 1.4 fusion.14
  49.7 35.8 %reduce-scatter.7.cloned.1.call-done = f32[128,256]{0,1:T(8,128)} async-done(((f32[1024,256]{0,1:T(8,128)}), f32[128,256]{0,1:T(8,128)}) %reduce-scatter.7.cloned.1.call-update) | async-done | bytes 131088 | tf_op jit(solution)/shard_map/reduce_scatter | solution.py:83
  85.5 0.9 convert_element_type.45
  86.4 0.7 pad_maximum_fusion.1
  87.2 0.7 all-gather.5.cloned.1.call-update
  87.9 1.4 copy.53
  89.3 3.7 %all-to-all-start = ((bf16[128,8,640]{0,2,1:T(8,128)(2,1)}), bf16[128,8,640]{0,2,1:T(8,128)(2,1)S(1)}, u32[]{:S(2)}, u32[]{:S(2)}) async-start(bf16[128,8,640]{0,2,1:T(8,128)(2,1)} %bitcast.23), calls=%async_computation.1 | async-start | bytes 2621440 | tf_op jit(solution)/shard_map/all_to_all | solution.py:90
  93.0 0.2 copy.80
  93.3 1.2 copy.55
  94.5 19.2 %all-to-all-done = bf16[128,8,640]{0,2,1:T(8,128)(2,1)S(1)} async-done(((bf16[128,8,640]{0,2,1:T(8,128)(2,1)}), bf16[128,8,640]{0,2,1:T(8,128)(2,1)S(1)}, u32[]{:S(2)}, u32[]{:S(2)}) %all-to-all-start) | async-done | bytes 1310752 | tf_op jit(solution)/shard_map/all_to_all | solution.py:90
  113.7 3.6 %all-to-all-start.1 = ((bf16[128,8,640]{2,0,1:T(8,128)(2,1)}), bf16[128,8,640]{2,0,1:T(8,128)(2,1)S(1)}, u32[]{:S(2)}, u32[]{:S(2)}) async-start(bf16[128,8,640]{2,0,1:T(8,128)(2,1)} %copy.55), calls=%async_computation.2 | async-start | bytes 2621440 | tf_op jit(solution)/shard_map/all_to_all | solution.py:91
  117.3 1.5 copy.54
  118.8 1.6 all-gather.3.cloned.1.call-done
  120.4 4.8 %convolution_bitcast_fusion = f32[640,896]{0,1:T(8,128)} fusion(bf16[1024,896]{0,1:T(8,128)(2,1)} %all-gather.3.cloned.1.call-done, bf16[1024,640]{1,0:T(8,128)(2,1)} %bitcast.113), kind=kOutput, calls=%fused_computation.11 | convolution fusion | flops 1174405120 | bytes 5439488 | tf_op jit(solution)/shard_map/dot_general | solution.py:97
  125.3 3.2 %copy.76 = f32[640,896]{1,0:T(8,128)} copy(f32[640,896]{0,1:T(8,128)} %convolution_bitcast_fusion) | data formatting | bytes 4587520
  128.5 8.6 %all-to-all-done.1 = bf16[128,8,640]{2,0,1:T(8,128)(2,1)S(1)} async-done(((bf16[128,8,640]{2,0,1:T(8,128)(2,1)}), bf16[128,8,640]{2,0,1:T(8,128)(2,1)S(1)}, u32[]{:S(2)}, u32[]{:S(2)}) %all-to-all-start.1) | async-done | bytes 1310752 | tf_op jit(solution)/shard_map/all_to_all | solution.py:91
  137.1 11.4 %all-gather.5.cloned.1.call-done = bf16[1024,640]{0,1:T(8,128)(2,1)} async-done(((bf16[128,640]{0,1:T(8,128)(2,1)}), bf16[1024,640]{0,1:T(8,128)(2,1)}) %all-gather.5.cloned.1.call-update) | async-done | bytes 1310736 | tf_op jit(solution)/shard_map/all_gather | solution.py:95
  148.5 2.5 %fusion.43 = f32[8,80,640]{2,1,0:T(8,128)S(1)} fusion(bf16[8,80,1024]{2,1,0:T(8,128)(2,1)} %bitcast.116, bf16[1024,640,1]{1,0,2:T(8,128)(2,1)S(1)} %bitcast.112), kind=kOutput, calls=%fused_computation.72 | convolution fusion | flops 838860800 | bytes 4259840 | tf_op jit(solution)/shard_map/dot_general | solution.py:100
  151.0 24.2 %all_to_all.54 = f32[8,80,640]{2,1,0:T(8,128)S(1)} all-to-all(f32[8,80,640]{2,1,0:T(8,128)S(1)} %fusion.43), channel_id=1, replica_groups=mesh['seq'=8,'dp'=4] {'seq'}, dimensions={0} | all-to-all | bytes 3276800 | tf_op jit(solution)/shard_map/all_to_all | solution.py:103
  175.4 54.7 %fusion = f32[24,5120]{1,0:T(8,128)S(1)} fusion(f32[80,5120]{1,0:T(8,128)S(1)} %bitcast.101), kind=kCustom, calls=%all-reduce-scatter | all-reduce-scatter fusion | flops 491521 | bytes 2130432
  230.1 1.3 collective-permute-start.7
  231.4 0.6 dynamic-slice.7
  232.7 5.7 %collective-permute-done.7 = f32[12,5120]{1,0:T(8,128)S(1)} collective-permute-done((f32[12,5120]{1,0:T(8,128)S(1)}, f32[12,5120]{1,0:T(8,128)S(1)}, u32[]{:S(2)}, u32[]{:S(2)}) %collective-permute-start.7) | collective-permute-done | bytes 245792
  238.3 0.5 concatenate.19
  238.9 0.8 constant_dynamic-slice_fusion
  (50 shorter events, 0.6 us)
Async XLA Ops:
  7.2 3.4 %copy-start = (bf16[1,128,5120]{2,1,0:T(8,128)(2,1)S(1)}, bf16[1,128,5120]{2,1,0:T(8,128)(2,1)}, u32[]{:S(2)}) copy-start(bf16[1,128,5120]{2,1,0:T(8,128)(2,1)} %param.7) | copy-start | bytes 3932164
  7.2 78.3 %reduce-scatter.7.cloned.1.call-start = ((), (), s32[]{:S(2)}) async-start(), calls=%async_computation.5 | async-start | bytes 1179648 | tf_op jit(solution)/shard_map/reduce_scatter | solution.py:83
  7.2 10.0 %slice-start = ((s8[6553600]{0:T(1024)(128)(4,1)}), s8[4194304]{0:T(1024)(128)(4,1)S(1)}, s32[]{:S(2)}) async-start(s8[6553600]{0:T(1024)(128)(4,1)} %bitcast.102), calls=%async_computation.9 | async-start | bytes 8388608
  10.0 7.3 %slice-start.1 = ((s8[6553600]{0:T(1024)(128)(4,1)}), s8[2359296]{0:T(1024)(128)(4,1)S(1)}, s32[]{:S(2)}) async-start(s8[6553600]{0:T(1024)(128)(4,1)} %bitcast.102), calls=%async_computation.10 | async-start | bytes 4718592
  10.0 7.2 %copy-start.1 = (bf16[1,128,5120]{2,1,0:T(8,128)(2,1)S(1)}, bf16[1,128,5120]{2,1,0:T(8,128)(2,1)}, u32[]{:S(2)}) copy-start(bf16[1,128,5120]{2,1,0:T(8,128)(2,1)} %param.8) | copy-start | bytes 3932164
  10.0 5.3 %collective-permute-start = (bf16[128,256]{1,0:T(8,128)(2,1)S(1)}, bf16[128,256]{1,0:T(8,128)(2,1)S(1)}, u32[]{:S(2)}, u32[]{:S(2)}) collective-permute-start(bf16[128,256]{1,0:T(8,128)(2,1)S(1)} %fusion.26), channel_id=1, source_target_pairs={{0,4},{4,8},{8,12},{12,16},{16,20},{20,24},{24,28},{28,0},{1,5},{5... | collective-permute-start | bytes 196616 | tf_op jit(solution)/shard_map/ppermute | solution.py:14
  15.4 4.6 %collective-permute-start.1 = (bf16[128,256]{1,0:T(8,128)(2,1)S(1)}, bf16[128,256]{1,0:T(8,128)(2,1)S(1)}, u32[]{:S(2)}, u32[]{:S(2)}) collective-permute-start(bf16[128,256]{1,0:T(8,128)(2,1)S(1)} %collective-permute-done), channel_id=1, source_target_pairs={{0,4},{4,8},{8,12},{12,16},{16,20},{20,24},{24,28},{28,0},{1,5},{5... | collective-permute-start | bytes 196616 | tf_op jit(solution)/shard_map/ppermute | solution.py:14
  20.0 4.6 %collective-permute-start.2 = (bf16[128,256]{1,0:T(8,128)(2,1)S(1)}, bf16[128,256]{1,0:T(8,128)(2,1)S(1)}, u32[]{:S(2)}, u32[]{:S(2)}) collective-permute-start(bf16[128,256]{1,0:T(8,128)(2,1)S(1)} %collective-permute-done.1), channel_id=1, source_target_pairs={{0,4},{4,8},{8,12},{12,16},{16,20},{20,24},{24,28},{28,0},{1,5},{5... | collective-permute-start | bytes 196616 | tf_op jit(solution)/shard_map/ppermute | solution.py:14
  24.5 4.6 %collective-permute-start.3 = (bf16[128,256]{1,0:T(8,128)(2,1)S(1)}, bf16[128,256]{1,0:T(8,128)(2,1)S(1)}, u32[]{:S(2)}, u32[]{:S(2)}) collective-permute-start(bf16[128,256]{1,0:T(8,128)(2,1)S(1)} %collective-permute-done.2), channel_id=1, source_target_pairs={{0,4},{4,8},{8,12},{12,16},{16,20},{20,24},{24,28},{28,0},{1,5},{5... | collective-permute-start | bytes 196616 | tf_op jit(solution)/shard_map/ppermute | solution.py:14
  29.1 4.6 %collective-permute-start.4 = (bf16[128,256]{1,0:T(8,128)(2,1)S(1)}, bf16[128,256]{1,0:T(8,128)(2,1)S(1)}, u32[]{:S(2)}, u32[]{:S(2)}) collective-permute-start(bf16[128,256]{1,0:T(8,128)(2,1)S(1)} %collective-permute-done.3), channel_id=1, source_target_pairs={{0,4},{4,8},{8,12},{12,16},{16,20},{20,24},{24,28},{28,0},{1,5},{5... | collective-permute-start | bytes 196616 | tf_op jit(solution)/shard_map/ppermute | solution.py:14
  33.7 4.6 %collective-permute-start.5 = (bf16[128,256]{1,0:T(8,128)(2,1)S(1)}, bf16[128,256]{1,0:T(8,128)(2,1)S(1)}, u32[]{:S(2)}, u32[]{:S(2)}) collective-permute-start(bf16[128,256]{1,0:T(8,128)(2,1)S(1)} %collective-permute-done.4), channel_id=1, source_target_pairs={{0,4},{4,8},{8,12},{12,16},{16,20},{20,24},{24,28},{28,0},{1,5},{5... | collective-permute-start | bytes 196616 | tf_op jit(solution)/shard_map/ppermute | solution.py:14
  38.3 4.6 %collective-permute-start.6 = (bf16[128,256]{1,0:T(8,128)(2,1)S(1)}, bf16[128,256]{1,0:T(8,128)(2,1)S(1)}, u32[]{:S(2)}, u32[]{:S(2)}) collective-permute-start(bf16[128,256]{1,0:T(8,128)(2,1)S(1)} %collective-permute-done.5), channel_id=1, source_target_pairs={{0,4},{4,8},{8,12},{12,16},{16,20},{20,24},{24,28},{28,0},{1,5},{5... | collective-permute-start | bytes 196616 | tf_op jit(solution)/shard_map/ppermute | solution.py:14
  43.1 2.8 %copy-start.3 = (bf16[2048,256]{1,0:T(8,128)(2,1)}, bf16[2048,256]{1,0:T(8,128)(2,1)S(1)}, u32[]{:S(2)}) copy-start(bf16[2048,256]{1,0:T(8,128)(2,1)S(1)} %constant_dynamic-update-slice_fusion) | copy-start | bytes 3145732
  48.3 72.2 %all-gather.3.cloned.1.call-start = ((), (), s32[]{:S(2)}) async-start(), calls=%async_computation.6 | async-start | bytes 2064384 | tf_op jit(solution)/shard_map/all_gather | solution.py:94
  87.1 61.4 %all-gather.5.cloned.1.call-start = ((), (), s32[]{:S(2)}) async-start(), calls=%async_computation.7 | async-start | bytes 1474560 | tf_op jit(solution)/shard_map/all_gather | solution.py:95
  89.3 3.7 %copy-start.2 = (bf16[1,128,5120]{2,1,0:T(8,128)(2,1)S(1)}, bf16[1,128,5120]{2,1,0:T(8,128)(2,1)}, u32[]{:S(2)}) copy-start(bf16[1,128,5120]{2,1,0:T(8,128)(2,1)} %param.8) | copy-start | bytes 3932164
  89.3 24.3 %all-to-all-start = ((bf16[128,8,640]{0,2,1:T(8,128)(2,1)}), bf16[128,8,640]{0,2,1:T(8,128)(2,1)S(1)}, u32[]{:S(2)}, u32[]{:S(2)}) async-start(bf16[128,8,640]{0,2,1:T(8,128)(2,1)} %bitcast.23), calls=%async_computation.1 | async-start | bytes 2621440 | tf_op jit(solution)/shard_map/all_to_all | solution.py:90
  113.7 23.5 %all-to-all-start.1 = ((bf16[128,8,640]{2,0,1:T(8,128)(2,1)}), bf16[128,8,640]{2,0,1:T(8,128)(2,1)S(1)}, u32[]{:S(2)}, u32[]{:S(2)}) async-start(bf16[128,8,640]{2,0,1:T(8,128)(2,1)} %copy.55), calls=%async_computation.2 | async-start | bytes 2621440 | tf_op jit(solution)/shard_map/all_to_all | solution.py:91
  117.2 122.4 %reduce-scatter.9.cloned.1.call-start = ((), (), s32[]{:S(2)}) async-start(), calls=%async_computation.8 | async-start | bytes 2867200
  175.4 56.1 %copy-start.4 = (u32[32]{0:T(128)S(1)}, u32[32]{0:T(128)}, u32[]{:S(2)}) copy-start(u32[32]{0:T(128)} %constant.84) | copy-start | bytes 388
  230.1 8.2 %collective-permute-start.7 = (f32[12,5120]{1,0:T(8,128)S(1)}, f32[12,5120]{1,0:T(8,128)S(1)}, u32[]{:S(2)}, u32[]{:S(2)}) collective-permute-start(f32[12,5120]{1,0:T(8,128)S(1)} %slice.8), channel_id=1, source_target_pairs={{0,1},{1,2},{2,3},{4,5},{5,6},{6,7},{8,9},{9,10},{10,11},{12,13},{... | collective-permute-start | bytes 737288
Sparse Core Ops, SparseCore 0:
  48.4 37.0 reduce-scatter.6
  88.0 32.4 all-gather.2
  122.3 26.1 all-gather.4
  151.3 59.2 reduce-scatter.8
